TPU v7x, 256 devices: a whole 4x4x8 slice. The times are simulated.
256 devices in a mesh: band: 8 (over y, core), plane: 32 (over x, z).
Axes of the slice: x: 4, y: 4, z: 8, core: 2. Of those that a mesh axis runs over, the one named last changes fastest.
Arguments:
- psi: float32 [2, 8, 4096, 128], P(None, 'band', 'plane'), may hold values from -8 to 8
- potential: float32 [96, 9216], P('plane'), may hold values from 0 to 2
- stick_column: int32 [4096], P('plane'), may hold values from 0 to 9215, as said below
- stick_length: int32 [4096], P('plane'), may hold values from 0 to 49, as said below
Outputs:
- psi_new: float32 [2, 8, 4096, 128], P(None, 'band', 'plane')
- potential_new: float32 [96, 9216], P('plane')
Inputs may be any that keep to these rules, and one draw needn't show every extreme that they name: `stick_column`: within each device's block of 128 slots the live sticks come first and the other slots are empty with column 0. Over all devices the live slots hold every column (mx mod 96) * 96 + (my mod 96) with mx * mx + my * my <= 576 exactly once, in an order drawn from the seed; some device's block is full and the others hold fewer. `stick_length`: A live slot's length is 2 h + 1, with h the largest whole number such that mx * mx + my * my + h * h <= 576 for its column; empty slots have length 0.
All inputs are finite; a program needn't handle non-finite values.
Results may differ from a plain program's by a relative error of at most 0.0001.
Values sent between devices are 32-bit elements; how exact they have to be, the bound alone decides.
No kernel may reach another device: no remote copies, remote signals or barrier semaphores. Data moves between devices by JAX's collectives and lax.ppermute only.
A program may use at most 64 MiB of HBM per device.

v0:
```python
import math
import jax
import jax.numpy as jnp
from jax import lax
from jax.sharding import PartitionSpec as P

NG = 96
RAD = 24
STICK_COEFFS = 128
BAND_DEV = 1
HIGHEST = lax.Precision.HIGHEST
TIMESTEP = 0.6
LINEAR_GAIN = 0.5
CUBIC_GAIN = 0.3


def turning(values):
    return values.astype(jnp.float32) * (2.0 * math.pi / NG)


def height_tables(lengths, columns, planes, device_list):
    order = jnp.arange(STICK_COEFFS, dtype=jnp.int32)
    height = (
        jnp.arange(device_list, dtype=jnp.int32)[None, :] * planes
        + jnp.arange(planes, dtype=jnp.int32)[:, None]
    )
    scale = NG ** (-0.5)
    wave_angle = turning(order[:, None, None] * height[None, :, :] % NG)
    wave = (jnp.cos(wave_angle) * scale, jnp.sin(wave_angle) * scale)
    half = (lengths - 1) // 2
    shift_angle = -turning(height[:, :, None] * half[None, None, :] % NG)
    shift = (jnp.cos(shift_angle), jnp.sin(shift_angle))
    mask = (order[None, :] < lengths[:, None]).astype(jnp.float32)
    first = columns // NG
    second = columns % NG
    first = jnp.where(first > NG // 2, first - NG, first)
    second = jnp.where(second > NG // 2, second - NG, second)
    depth = order[None, :] - half[:, None]
    kinetic = (
        ((first * first + second * second)[:, None] + depth * depth).astype(jnp.float32)
        / (RAD * RAD)
        * mask
    )
    return (wave, shift, mask, kinetic)


def along_height(terms, tables):
    wave, shift = (tables[0], tables[1])

    def contract(left, right):
        return jnp.einsum("bsj,jdn->bdns", left, right, precision=HIGHEST)

    upper_real = contract(terms[0], wave[0]) - contract(terms[1], wave[1])
    upper_imag = contract(terms[0], wave[1]) + contract(terms[1], wave[0])
    return jnp.stack(
        [
            upper_real * shift[0] - upper_imag * shift[1],
            upper_real * shift[1] + upper_imag * shift[0],
        ]
    )


def from_height(values, tables):
    wave, shift, mask = (tables[0], tables[1], tables[2])
    turned_real = values[0] * shift[0] + values[1] * shift[1]
    turned_imag = values[1] * shift[0] - values[0] * shift[1]

    def contract(left, right):
        return jnp.einsum("bdns,jdn->bsj", left, right, precision=HIGHEST)

    real_part = contract(turned_real, wave[0]) + contract(turned_imag, wave[1])
    imag_part = contract(turned_imag, wave[0]) - contract(turned_real, wave[1])
    return jnp.stack([real_part * mask, imag_part * mask])


def plane_tables():
    index = jnp.arange(NG, dtype=jnp.int32)
    angle = turning(index[:, None] * index[None, :] % NG)
    scale = NG ** (-0.5)
    return (jnp.cos(angle) * scale, jnp.sin(angle) * scale)


def plane_transform(values, cosine, sine):
    bands, planes = (values.shape[1], values.shape[2])
    real_part = values[0].reshape(bands, planes, NG, NG)
    imag_part = values[1].reshape(bands, planes, NG, NG)

    def inner(left, right):
        return jnp.einsum("bdmk,ky->bdmy", left, right, precision=HIGHEST)

    def outer(left, right):
        return jnp.einsum("mx,bdmy->bdxy", left, right, precision=HIGHEST)

    middle_real = inner(real_part, cosine) - inner(imag_part, sine)
    middle_imag = inner(real_part, sine) + inner(imag_part, cosine)
    final_real = outer(cosine, middle_real) - outer(sine, middle_imag)
    final_imag = outer(sine, middle_real) + outer(cosine, middle_imag)
    return jnp.stack([final_real, final_imag]).reshape(2, bands, planes, NG * NG)


def cell_slots(columns, lengths):
    count = columns.shape[0]
    target = jnp.where(lengths > 0, columns, NG * NG)
    table = jnp.full((NG * NG,), -1, jnp.int32)
    return table.at[target].set(jnp.arange(count, dtype=jnp.int32), mode="drop")


def spread_columns(values, table):
    picked = jnp.take(values, jnp.maximum(table, 0), axis=3)
    return jnp.where(table >= 0, picked, 0.0)


def modulus(field):
    return jnp.sum(field[0] * field[0] + field[1] * field[1], axis=0)


def advance(applied, power):
    factor = TIMESTEP / power
    return jnp.stack([factor * applied[1], -factor * applied[0]])


def shards(psi, potential, stick_column, stick_length):
    device_list = lax.axis_size("plane")
    planes = potential.shape[0]
    slots = stick_column.shape[0]
    bands = psi.shape[1]
    cosine, sine = plane_tables()
    own = height_tables(stick_length, stick_column, planes, device_list)
    term = psi * own[2]
    columns, lengths = (
        lax.all_gather(stick_column, "plane", axis=0, tiled=True),
        lax.all_gather(stick_length, "plane", axis=0, tiled=True),
    )
    given_cells = cell_slots(columns, lengths)
    total = term
    before = jnp.zeros((planes, NG * NG), jnp.float32)
    for power in range(1, 4):
        arrived = lax.all_to_all(
            along_height(term, own), "plane", split_axis=3, concat_axis=3, tiled=True
        ).reshape(2, bands, planes, device_list * slots)
        field = plane_transform(spread_columns(arrived, given_cells), cosine, sine)
        if power == 1:
            before = modulus(field)
        spectrum = plane_transform(field * potential, cosine, -sine)
        picked = spectrum[:, :, :, columns].reshape(2, bands, planes, device_list, slots)
        returned = lax.all_to_all(picked, "plane", split_axis=3, concat_axis=3, tiled=True)
        term = advance(from_height(returned, own) + own[3] * term, power)
        total = total + term
    arrived = lax.all_to_all(
        along_height(total, own), "plane", split_axis=3, concat_axis=3, tiled=True
    ).reshape(2, bands, planes, device_list * slots)
    after = modulus(plane_transform(spread_columns(arrived, given_cells), cosine, sine))
    change = (after - before) / BAND_DEV
    whole = lax.psum(change, "band")
    potential_new = potential + LINEAR_GAIN * whole + CUBIC_GAIN * whole * whole * whole
    return (total, potential_new)


def solution(mesh):
    in_specs = (P(None, "band", "plane", None), P("plane", None), P("plane"), P("plane"))
    out_specs = (P(None, "band", "plane", None), P("plane", None))
    return jax.shard_map(shards, mesh=mesh, in_specs=in_specs, out_specs=out_specs, check_vma=False)
```

profile of v0, /device:TPU:2, one launch (start us, length us, event | category | flops | bytes accessed | tf_op | source)
XLA Modules:
  0.0 968.3 jit_solution(16766717710354045417)
XLA Ops:
  12.2 11.6 %all-to-all-start = ((f32[2,1,3,32,128]{4,0,2,1,3:T(2,128)}), f32[2,1,3,32,128]{4,0,2,1,3:T(2,128)S(1)}, u32[]{:S(2)}, u32[]{:S(2)}) async-start(f32[2,1,3,32,128]{4,0,2,1,3:T(2,128)} %copy.177), calls=%async_computation | async-start | bytes 196608 | tf_op jit(solution)/shard_map/all_to_all | solution.py:138
  23.8 39.6 %all-gather = s32[32,1,128]{2,1,0:T(1,128)S(1)} all-gather(s32[1,1,128]{2,1,0:T(1,128)} %bitcast.566), channel_id=1, replica_groups=mesh['band'=8,'plane'=32] {'plane'}, dimensions={0}, use_global_device_ids=true | all-gather | bytes 16896 | tf_op jit(solution)/shard_map/all_gather | solution.py:132
  63.4 36.7 %all-gather.1 = s32[32,1,128]{2,1,0:T(1,128)S(1)} all-gather(s32[1,1,128]{2,1,0:T(1,128)} %bitcast.567), channel_id=1, replica_groups=mesh['band'=8,'plane'=32] {'plane'}, dimensions={0}, use_global_device_ids=true | all-gather | bytes 16896 | tf_op jit(solution)/shard_map/all_gather | solution.py:131
  100.1 15.5 %scatter_custom_fusion = s32[9216]{0:T(1024)S(1)} fusion(s32[4096]{0:T(1024)S(1)} %get-tuple-element.40, s32[4096]{0:T(1024)S(1)} %iota.105, s32[]{:T(128)} %constant.56.clone.1), kind=kCustom, calls=%fused_computation.291 | custom fusion | bytes 36868 | tf_op jit(solution)/shard_map/scatter | solution.py:105
  116.4 4.3 copy.179
  120.7 65.0 %gather_fusion.3 = f32[9216,2,3]{2,1,0:T(2,128)} fusion(f32[2,3,4096]{1,0,2:T(2,128)} %bitcast.554, s32[9216]{0:T(1024)S(1)} %maximum_clamp_fusion), kind=kCustom, calls=%fused_computation.clone | custom fusion | bytes 479232 | tf_op jit(solution)/shard_map/jit(_take)/gather | solution.py:109
  185.7 42.6 %fusion.3 = f32[2,1,3,9216]{2,0,3,1:T(2,128)S(1)} fusion(f32[9216,2,3]{2,1,0:T(2,128)} %gather_fusion.3, pred[9216]{0:T(1024)(128)(4,1)S(1)} %get-tuple-element.38, pred[9216]{0:T(1024)(128)(4,1)S(1)} %get-tuple-element.37), kind=kLoop, calls=%fused_computation.15 | loop fusion | flops 110592 | bytes 460800 | tf_op jit(solution)/shard_map/jit(_where)/select_n | solution.py:110
  228.3 8.5 fusion.517
  236.8 3.1 copy.281
  240.9 3.6 copy.282
  254.3 8.9 copy.194
  263.2 31.8 %gather_fusion = f32[4096,2,3]{2,1,0:T(2,128)} fusion(f32[2,3,9216]{1,0,2:T(2,128)} %bitcast.550, s32[4096]{0:T(1024)S(1)} %get-tuple-element.39), kind=kCustom, calls=%fused_computation.4 | custom fusion | bytes 212992 | tf_op jit(solution)/shard_map/gather | solution.py:145
  295.1 5.8 copy.196
  300.9 6.5 all-to-all-start.1
  307.5 8.7 all-to-all-done.1
  321.1 13.5 %all_to_all.35 = f32[2,1,3,32,128]{4,0,2,1,3:T(2,128)S(1)} all-to-all(f32[2,1,3,32,128]{4,0,2,1,3:T(2,128)S(1)} %copy.199), channel_id=1, replica_groups=mesh['band'=8,'plane'=32] {'plane'}, dimensions={3} | all-to-all | bytes 196608 | tf_op jit(solution)/shard_map/all_to_all | solution.py:138
  334.6 4.3 copy.201
  339.0 65.0 %gather_fusion.4 = f32[9216,2,3]{2,1,0:T(2,128)} fusion(f32[2,3,4096]{1,0,2:T(2,128)} %bitcast.555, s32[9216]{0:T(1024)S(1)} %maximum_clamp_fusion), kind=kCustom, calls=%fused_computation.1.clone | custom fusion | bytes 479232 | tf_op jit(solution)/shard_map/jit(_take)/gather | solution.py:109
  403.9 42.6 %fusion.2 = f32[2,1,3,9216]{2,0,3,1:T(2,128)S(1)} fusion(f32[9216,2,3]{2,1,0:T(2,128)} %gather_fusion.4, pred[9216]{0:T(1024)(128)(4,1)S(1)} %get-tuple-element.38, pred[9216]{0:T(1024)(128)(4,1)S(1)} %get-tuple-element.37), kind=kLoop, calls=%fused_computation.13 | loop fusion | flops 110592 | bytes 460800 | tf_op jit(solution)/shard_map/jit(_where)/select_n | solution.py:110
  446.5 8.5 fusion.516
  455.0 3.1 copy.285
  459.1 3.3 copy.286
  472.2 8.9 copy.216
  481.1 31.8 %gather_fusion.1 = f32[4096,2,3]{2,1,0:T(2,128)} fusion(f32[2,3,9216]{1,0,2:T(2,128)} %bitcast.552, s32[4096]{0:T(1024)S(1)} %get-tuple-element.39), kind=kCustom, calls=%fused_computation.5 | custom fusion | bytes 212992 | tf_op jit(solution)/shard_map/gather | solution.py:145
  513.0 5.8 copy.218
  518.8 5.5 all-to-all-start.3
  524.3 8.9 all-to-all-done.3
  538.1 13.5 %all_to_all.36 = f32[2,1,3,32,128]{4,0,2,1,3:T(2,128)S(1)} all-to-all(f32[2,1,3,32,128]{4,0,2,1,3:T(2,128)S(1)} %copy.221), channel_id=1, replica_groups=mesh['band'=8,'plane'=32] {'plane'}, dimensions={3} | all-to-all | bytes 196608 | tf_op jit(solution)/shard_map/all_to_all | solution.py:138
  551.6 4.3 copy.223
  556.0 65.0 %gather_fusion.5 = f32[9216,2,3]{2,1,0:T(2,128)} fusion(f32[2,3,4096]{1,0,2:T(2,128)} %bitcast.556, s32[9216]{0:T(1024)S(1)} %maximum_clamp_fusion), kind=kCustom, calls=%fused_computation.2.clone | custom fusion | bytes 479232 | tf_op jit(solution)/shard_map/jit(_take)/gather | solution.py:109
  620.9 42.6 %fusion.1 = f32[2,1,3,9216]{2,0,3,1:T(2,128)S(1)} fusion(f32[9216,2,3]{2,1,0:T(2,128)} %gather_fusion.5, pred[9216]{0:T(1024)(128)(4,1)S(1)} %get-tuple-element.38, pred[9216]{0:T(1024)(128)(4,1)S(1)} %get-tuple-element.37), kind=kLoop, calls=%fused_computation.11 | loop fusion | flops 110592 | bytes 460800 | tf_op jit(solution)/shard_map/jit(_where)/select_n | solution.py:110
  663.5 8.5 fusion.515
  672.0 3.1 copy.289
  676.1 3.3 copy.290
  689.2 8.9 copy.238
  698.1 31.8 %gather_fusion.2 = f32[4096,2,3]{2,1,0:T(2,128)} fusion(f32[2,3,9216]{1,0,2:T(2,128)} %bitcast.551, s32[4096]{0:T(1024)S(1)} %get-tuple-element.39), kind=kCustom, calls=%fused_computation.6 | custom fusion | bytes 212992 | tf_op jit(solution)/shard_map/gather | solution.py:145
  729.9 5.8 copy.240
  735.8 5.0 all-to-all-start.5
  741.0 8.8 all-to-all-done.5
  754.8 13.5 %all_to_all.37 = f32[2,1,3,32,128]{4,0,2,1,3:T(2,128)S(1)} all-to-all(f32[2,1,3,32,128]{4,0,2,1,3:T(2,128)S(1)} %copy.243), channel_id=1, replica_groups=mesh['band'=8,'plane'=32] {'plane'}, dimensions={3} | all-to-all | bytes 196608 | tf_op jit(solution)/shard_map/all_to_all | solution.py:149
  768.3 4.3 copy.245
  772.6 65.0 %gather_fusion.6 = f32[9216,2,3]{2,1,0:T(2,128)} fusion(f32[2,3,4096]{1,0,2:T(2,128)} %bitcast.553, s32[9216]{0:T(1024)S(1)} %maximum_clamp_fusion), kind=kCustom, calls=%fused_computation.3.clone | custom fusion | bytes 479232 | tf_op jit(solution)/shard_map/jit(_take)/gather | solution.py:109
  837.6 42.6 %fusion = f32[2,1,3,9216]{2,0,3,1:T(2,128)S(1)} fusion(f32[9216,2,3]{2,1,0:T(2,128)} %gather_fusion.6, pred[9216]{0:T(1024)(128)(4,1)S(1)} %get-tuple-element.38, pred[9216]{0:T(1024)(128)(4,1)S(1)} %get-tuple-element.37), kind=kLoop, calls=%fused_computation.9 | loop fusion | flops 110592 | bytes 460800 | tf_op jit(solution)/shard_map/jit(_where)/select_n | solution.py:110
  880.2 8.5 fusion.514
  888.7 3.1 copy.293
  892.8 3.1 copy.294
  899.9 59.6 %all-reduce.2.cloned.1.call-done = f32[3,9216]{1,0:T(4,128)} async-done(((f32[3,9216]{1,0:T(4,128)}), f32[3,9216]{1,0:T(4,128)}) %all-reduce.2.cloned.1.call-update) | async-done | bytes 110608 | tf_op jit(solution)/shard_map/psum | solution.py:154
  959.6 1.6 fusion.39
  (169 shorter events, 57.4 us)
Async XLA Ops:
  12.2 104.2 %all-to-all-start = ((f32[2,1,3,32,128]{4,0,2,1,3:T(2,128)}), f32[2,1,3,32,128]{4,0,2,1,3:T(2,128)S(1)}, u32[]{:S(2)}, u32[]{:S(2)}) async-start(f32[2,1,3,32,128]{4,0,2,1,3:T(2,128)} %copy.177), calls=%async_computation | async-start | bytes 196608 | tf_op jit(solution)/shard_map/all_to_all | solution.py:138
  236.8 11.4 %copy-start = (f32[3,9216]{1,0:T(4,128)S(1)}, f32[3,9216]{1,0:T(4,128)}, u32[]{:S(2)}) copy-start(f32[3,9216]{1,0:T(4,128)} %param.7) | copy-start | bytes 331780
  249.7 57.6 %copy-start.3 = (s32[128]{0:T(128)S(1)}, s32[128]{0:T(128)}, u32[]{:S(2)}) copy-start(s32[128]{0:T(128)} %param.9) | copy-start | bytes 1540
  252.4 66.7 %copy-start.1 = (f32[2,1,128,128]{3,2,1,0:T(8,128)S(1)}, f32[2,1,128,128]{3,2,1,0:T(8,128)}, u32[]{:S(2)}) copy-start(f32[2,1,128,128]{3,2,1,0:T(8,128)} %param.6) | copy-start | bytes 393220
  300.9 15.3 %all-to-all-start.1 = ((f32[2,1,3,32,128]{4,0,2,1,3:T(2,128)}), f32[2,1,3,32,128]{4,0,2,1,3:T(2,128)S(1)}, u32[]{:S(2)}, u32[]{:S(2)}) async-start(f32[2,1,3,32,128]{4,0,2,1,3:T(2,128)} %copy.196), calls=%async_computation.1 | async-start | bytes 196608 | tf_op jit(solution)/shard_map/all_to_all | solution.py:146
  518.8 14.4 %all-to-all-start.3 = ((f32[2,1,3,32,128]{4,0,2,1,3:T(2,128)}), f32[2,1,3,32,128]{4,0,2,1,3:T(2,128)S(1)}, u32[]{:S(2)}, u32[]{:S(2)}) async-start(f32[2,1,3,32,128]{4,0,2,1,3:T(2,128)} %copy.218), calls=%async_computation.3 | async-start | bytes 196608 | tf_op jit(solution)/shard_map/all_to_all | solution.py:146
  735.8 14.0 %all-to-all-start.5 = ((f32[2,1,3,32,128]{4,0,2,1,3:T(2,128)}), f32[2,1,3,32,128]{4,0,2,1,3:T(2,128)S(1)}, u32[]{:S(2)}, u32[]{:S(2)}) async-start(f32[2,1,3,32,128]{4,0,2,1,3:T(2,128)} %copy.240), calls=%async_computation.5 | async-start | bytes 196608 | tf_op jit(solution)/shard_map/all_to_all | solution.py:146
  740.7 218.8 %all-reduce.2.cloned.1.call-start = ((), (), s32[]{:S(2)}) async-start(), calls=%async_computation.7 | async-start | bytes 294912 | tf_op jit(solution)/shard_map/psum | solution.py:154
  752.7 127.4 %copy-start.2 = (f32[2,1,128,128]{3,2,1,0:T(8,128)}, f32[2,1,128,128]{3,2,1,0:T(8,128)S(1)}, u32[]{:S(2)}) copy-start(f32[2,1,128,128]{3,2,1,0:T(8,128)S(1)} %maximum_add_fusion.3) | copy-start | bytes 393220
Sparse Core Ops, SparseCore 0:
  900.1 59.4 all-reduce.1
where the time goes:
time: 975 us; the launch traced here: 968 us
  local copies, waits for them, and re-layouts  501 us (51%)
  other arithmetic  177 us (18%)
  blocking collectives  117 us (12%)
  waiting for transfers between devices  86.1 us (9%)
  matrix products  43.7 us (4%)
  starting transfers between devices  28.8 us (3%)
  between operations  15.4 us (2%)
    gather x4, local copies, waits for them, and re-layouts, spread_columns(): picked = jnp.take(values, jnp.maximum(table, 0), axis=3)  260 us
    select_n x4, other arithmetic, spread_columns(): return jnp.where(table >= 0, picked, 0.0)  170 us
    gather x3, local copies, waits for them, and re-layouts, shards(): spectrum[:, :, :, columns].reshape(2, bands, planes, device_list, slots)  95.5 us
    psum x1, waiting for transfers between devices, shards(): whole = lax.psum(change, 'band')  59.6 us
    all_gather x1, blocking collectives, shards(): lax.all_gather(stick_length, 'plane', axis=0, tiled=True)  39.6 us
    all_gather x1, blocking collectives, shards(): lax.all_gather(stick_column, 'plane', axis=0, tiled=True)  36.7 us
    slice x7, local copies, waits for them, and re-layouts, plane_transform(): imag_part = values[1].reshape(bands, planes, NG, NG)  35.9 us
    another operation x15, local copies, waits for them, and re-layouts, plane_transform(): jnp.stack([final_real, final_imag]).reshape(2, bands, planes, NG * NG)  29.1 us
  transfers between devices with their start and end apart: 5, of which 4 were waited for; matrix products, arithmetic and copies ran while one was open for 2% of the time, Pallas kernels for 0%

commit v1 on v0

--- a/solution.py
+++ b/solution.py
@@ -151,7 +151,7 @@
     ).reshape(2, bands, planes, device_list * slots)
     after = modulus(plane_transform(spread_columns(arrived, given_cells), cosine, sine))
     change = (after - before) / BAND_DEV
-    whole = lax.psum(change, "band")
+    whole = jnp.sum(lax.all_gather(change, "band"), axis=0)
     potential_new = potential + LINEAR_GAIN * whole + CUBIC_GAIN * whole * whole * whole
     return (total, potential_new)
 

time: 975 us -> 921 us (0.945)
  waiting for transfers between devices: 86.1 us -> 26.6 us
  blocking collectives: 117 us -> 131 us
  between operations: 15.4 us -> 2.06 us
    psum x1 -> x0, waiting for transfers between devices: 59.6 us -> none  [shards(): whole = lax.psum(change, 'band')]
    all_gather x0 -> x1, blocking collectives: none -> 14.6 us  [shards(): whole = jnp.sum(lax.all_gather(change, 'band'), axis=0)]
  transfers between devices with their start and end apart: 5 -> 4, of which waited for: 4 -> 3; matrix products, arithmetic and copies ran while one was open for 2% -> 2% of each run, Pallas kernels for 0% -> 0%
where the time goes in v1:
time: 921 us; the launch traced here: 911 us
  local copies, waits for them, and re-layouts  503 us (55%)
  other arithmetic  176 us (19%)
  blocking collectives  131 us (14%)
  matrix products  43.8 us (5%)
  starting transfers between devices  28.8 us (3%)
  waiting for transfers between devices  26.6 us (3%)
    gather x4, local copies, waits for them, and re-layouts, spread_columns(): picked = jnp.take(values, jnp.maximum(table, 0), axis=3)  262 us
    select_n x4, other arithmetic, spread_columns(): return jnp.where(table >= 0, picked, 0.0)  170 us
    gather x3, local copies, waits for them, and re-layouts, shards(): spectrum[:, :, :, columns].reshape(2, bands, planes, device_list, slots)  96.1 us
    all_gather x1, blocking collectives, shards(): lax.all_gather(stick_length, 'plane', axis=0, tiled=True)  39.6 us
    all_gather x1, blocking collectives, shards(): lax.all_gather(stick_column, 'plane', axis=0, tiled=True)  36.7 us
    slice x7, local copies, waits for them, and re-layouts, plane_transform(): imag_part = values[1].reshape(bands, planes, NG, NG)  36 us
    another operation x15, local copies, waits for them, and re-layouts, plane_transform(): jnp.stack([final_real, final_imag]).reshape(2, bands, planes, NG * NG)  29.2 us
    all_to_all x2, blocking collectives, shards(): lax.all_to_all(along_height(term, own), 'plane', split_axis=3, concat_axi...  27 us
  transfers between devices with their start and end apart: 4, of which 3 were waited for; matrix products, arithmetic and copies ran while one was open for 2% of the time, Pallas kernels for 0%

profile of v1, /device:TPU:2, one launch (start us, length us, event | category | flops | bytes accessed | tf_op | source)
XLA Modules:
  0.0 911.4 jit_solution(13112511072491439660)
XLA Ops:
  2.1 0.9 broadcast_multiply_fusion
  5.7 11.6 %all-to-all-start = ((f32[2,1,3,32,128]{4,0,2,1,3:T(2,128)}), f32[2,1,3,32,128]{4,0,2,1,3:T(2,128)S(1)}, u32[]{:S(2)}, u32[]{:S(2)}) async-start(f32[2,1,3,32,128]{4,0,2,1,3:T(2,128)} %copy.178), calls=%async_computation | async-start | bytes 196608 | tf_op jit(solution)/shard_map/all_to_all | solution.py:138
  17.3 39.6 %all-gather = s32[32,1,128]{2,1,0:T(1,128)S(1)} all-gather(s32[1,1,128]{2,1,0:T(1,128)} %bitcast.568), channel_id=1, replica_groups=mesh['band'=8,'plane'=32] {'plane'}, dimensions={0}, use_global_device_ids=true | all-gather | bytes 16896 | tf_op jit(solution)/shard_map/all_gather | solution.py:132
  56.9 36.7 %all-gather.1 = s32[32,1,128]{2,1,0:T(1,128)S(1)} all-gather(s32[1,1,128]{2,1,0:T(1,128)} %bitcast.569), channel_id=1, replica_groups=mesh['band'=8,'plane'=32] {'plane'}, dimensions={0}, use_global_device_ids=true | all-gather | bytes 16896 | tf_op jit(solution)/shard_map/all_gather | solution.py:131
  93.6 15.5 %scatter_custom_fusion = s32[9216]{0:T(1024)S(1)} fusion(s32[4096]{0:T(1024)S(1)} %get-tuple-element.40, s32[4096]{0:T(1024)S(1)} %iota.105, s32[]{:T(128)} %constant.56.clone.1), kind=kCustom, calls=%fused_computation.291 | custom fusion | bytes 36868 | tf_op jit(solution)/shard_map/scatter | solution.py:105
  109.9 4.4 copy.180
  114.2 65.4 %gather_fusion.3 = f32[9216,2,3]{2,1,0:T(2,128)} fusion(f32[2,3,4096]{1,0,2:T(2,128)} %bitcast.556, s32[9216]{0:T(1024)S(1)} %maximum_clamp_fusion), kind=kCustom, calls=%fused_computation.clone | custom fusion | bytes 479232 | tf_op jit(solution)/shard_map/jit(_take)/gather | solution.py:109
  179.6 42.6 %fusion.3 = f32[2,1,3,9216]{2,0,3,1:T(2,128)S(1)} fusion(f32[9216,2,3]{2,1,0:T(2,128)} %gather_fusion.3, pred[9216]{0:T(1024)(128)(4,1)S(1)} %get-tuple-element.38, pred[9216]{0:T(1024)(128)(4,1)S(1)} %get-tuple-element.37), kind=kLoop, calls=%fused_computation.15 | loop fusion | flops 110592 | bytes 460800 | tf_op jit(solution)/shard_map/jit(_where)/select_n | solution.py:110
  222.2 8.5 fusion.517
  230.7 3.1 copy.283
  234.9 3.6 copy.284
  248.3 8.9 copy.195
  257.2 32.0 %gather_fusion = f32[4096,2,3]{2,1,0:T(2,128)} fusion(f32[2,3,9216]{1,0,2:T(2,128)} %bitcast.552, s32[4096]{0:T(1024)S(1)} %get-tuple-element.39), kind=kCustom, calls=%fused_computation.4 | custom fusion | bytes 212992 | tf_op jit(solution)/shard_map/gather | solution.py:145
  289.3 5.8 copy.197
  295.1 6.5 all-to-all-start.1
  301.7 8.7 all-to-all-done.1
  315.3 13.5 %all_to_all.35 = f32[2,1,3,32,128]{4,0,2,1,3:T(2,128)S(1)} all-to-all(f32[2,1,3,32,128]{4,0,2,1,3:T(2,128)S(1)} %copy.200), channel_id=1, replica_groups=mesh['band'=8,'plane'=32] {'plane'}, dimensions={3} | all-to-all | bytes 196608 | tf_op jit(solution)/shard_map/all_to_all | solution.py:138
  328.8 4.4 copy.202
  333.2 65.4 %gather_fusion.4 = f32[9216,2,3]{2,1,0:T(2,128)} fusion(f32[2,3,4096]{1,0,2:T(2,128)} %bitcast.557, s32[9216]{0:T(1024)S(1)} %maximum_clamp_fusion), kind=kCustom, calls=%fused_computation.1.clone | custom fusion | bytes 479232 | tf_op jit(solution)/shard_map/jit(_take)/gather | solution.py:109
  398.6 42.6 %fusion.2 = f32[2,1,3,9216]{2,0,3,1:T(2,128)S(1)} fusion(f32[9216,2,3]{2,1,0:T(2,128)} %gather_fusion.4, pred[9216]{0:T(1024)(128)(4,1)S(1)} %get-tuple-element.38, pred[9216]{0:T(1024)(128)(4,1)S(1)} %get-tuple-element.37), kind=kLoop, calls=%fused_computation.13 | loop fusion | flops 110592 | bytes 460800 | tf_op jit(solution)/shard_map/jit(_where)/select_n | solution.py:110
  441.2 8.5 fusion.516
  449.7 3.1 copy.287
  453.8 3.3 copy.288
  466.9 8.9 copy.217
  475.9 32.0 %gather_fusion.1 = f32[4096,2,3]{2,1,0:T(2,128)} fusion(f32[2,3,9216]{1,0,2:T(2,128)} %bitcast.554, s32[4096]{0:T(1024)S(1)} %get-tuple-element.39), kind=kCustom, calls=%fused_computation.5 | custom fusion | bytes 212992 | tf_op jit(solution)/shard_map/gather | solution.py:145
  507.9 5.8 copy.219
  513.7 5.5 all-to-all-start.3
  519.3 8.9 all-to-all-done.3
  533.1 13.5 %all_to_all.36 = f32[2,1,3,32,128]{4,0,2,1,3:T(2,128)S(1)} all-to-all(f32[2,1,3,32,128]{4,0,2,1,3:T(2,128)S(1)} %copy.222), channel_id=1, replica_groups=mesh['band'=8,'plane'=32] {'plane'}, dimensions={3} | all-to-all | bytes 196608 | tf_op jit(solution)/shard_map/all_to_all | solution.py:138
  546.6 4.4 copy.224
  550.9 65.4 %gather_fusion.5 = f32[9216,2,3]{2,1,0:T(2,128)} fusion(f32[2,3,4096]{1,0,2:T(2,128)} %bitcast.558, s32[9216]{0:T(1024)S(1)} %maximum_clamp_fusion), kind=kCustom, calls=%fused_computation.2.clone | custom fusion | bytes 479232 | tf_op jit(solution)/shard_map/jit(_take)/gather | solution.py:109
  616.4 42.6 %fusion.1 = f32[2,1,3,9216]{2,0,3,1:T(2,128)S(1)} fusion(f32[9216,2,3]{2,1,0:T(2,128)} %gather_fusion.5, pred[9216]{0:T(1024)(128)(4,1)S(1)} %get-tuple-element.38, pred[9216]{0:T(1024)(128)(4,1)S(1)} %get-tuple-element.37), kind=kLoop, calls=%fused_computation.11 | loop fusion | flops 110592 | bytes 460800 | tf_op jit(solution)/shard_map/jit(_where)/select_n | solution.py:110
  658.9 8.5 fusion.515
  667.5 3.1 copy.291
  671.5 3.3 copy.292
  684.6 8.9 copy.239
  693.6 32.0 %gather_fusion.2 = f32[4096,2,3]{2,1,0:T(2,128)} fusion(f32[2,3,9216]{1,0,2:T(2,128)} %bitcast.553, s32[4096]{0:T(1024)S(1)} %get-tuple-element.39), kind=kCustom, calls=%fused_computation.6 | custom fusion | bytes 212992 | tf_op jit(solution)/shard_map/gather | solution.py:145
  725.6 5.8 copy.241
  731.4 5.3 all-to-all-start.5
  736.7 8.9 all-to-all-done.5
  750.6 13.5 %all_to_all.37 = f32[2,1,3,32,128]{4,0,2,1,3:T(2,128)S(1)} all-to-all(f32[2,1,3,32,128]{4,0,2,1,3:T(2,128)S(1)} %copy.244), channel_id=1, replica_groups=mesh['band'=8,'plane'=32] {'plane'}, dimensions={3} | all-to-all | bytes 196608 | tf_op jit(solution)/shard_map/all_to_all | solution.py:149
  764.2 4.4 copy.246
  768.5 65.4 %gather_fusion.6 = f32[9216,2,3]{2,1,0:T(2,128)} fusion(f32[2,3,4096]{1,0,2:T(2,128)} %bitcast.555, s32[9216]{0:T(1024)S(1)} %maximum_clamp_fusion), kind=kCustom, calls=%fused_computation.3.clone | custom fusion | bytes 479232 | tf_op jit(solution)/shard_map/jit(_take)/gather | solution.py:109
  833.9 42.6 %fusion = f32[2,1,3,9216]{2,0,3,1:T(2,128)S(1)} fusion(f32[9216,2,3]{2,1,0:T(2,128)} %gather_fusion.6, pred[9216]{0:T(1024)(128)(4,1)S(1)} %get-tuple-element.38, pred[9216]{0:T(1024)(128)(4,1)S(1)} %get-tuple-element.37), kind=kLoop, calls=%fused_computation.9 | loop fusion | flops 110592 | bytes 460800 | tf_op jit(solution)/shard_map/jit(_where)/select_n | solution.py:110
  876.5 8.5 fusion.514
  885.0 3.1 copy.295
  889.1 3.1 copy.296
  895.6 14.6 %all_gather.12 = f32[8,3,9216]{2,1,0:T(4,128)S(1)} all-gather(f32[1,3,9216]{2,1,0:T(4,128)S(1)} %sub.249), channel_id=1, replica_groups=mesh['band'=8,'plane'=32] {'band'}, dimensions={0}, use_global_device_ids=true | all-gather | bytes 995328 | tf_op jit(solution)/shard_map/all_gather | solution.py:154
  (168 shorter events, 56.4 us)
Async XLA Ops:
  5.7 104.2 %all-to-all-start = ((f32[2,1,3,32,128]{4,0,2,1,3:T(2,128)}), f32[2,1,3,32,128]{4,0,2,1,3:T(2,128)S(1)}, u32[]{:S(2)}, u32[]{:S(2)}) async-start(f32[2,1,3,32,128]{4,0,2,1,3:T(2,128)} %copy.178), calls=%async_computation | async-start | bytes 196608 | tf_op jit(solution)/shard_map/all_to_all | solution.py:138
  230.7 11.4 %copy-start = (f32[3,9216]{1,0:T(4,128)S(1)}, f32[3,9216]{1,0:T(4,128)}, u32[]{:S(2)}) copy-start(f32[3,9216]{1,0:T(4,128)} %param.7) | copy-start | bytes 331780
  243.7 57.9 %copy-start.3 = (s32[128]{0:T(128)S(1)}, s32[128]{0:T(128)}, u32[]{:S(2)}) copy-start(s32[128]{0:T(128)} %param.9) | copy-start | bytes 1540
  246.4 66.9 %copy-start.1 = (f32[2,1,128,128]{3,2,1,0:T(8,128)S(1)}, f32[2,1,128,128]{3,2,1,0:T(8,128)}, u32[]{:S(2)}) copy-start(f32[2,1,128,128]{3,2,1,0:T(8,128)} %param.6) | copy-start | bytes 393220
  295.1 15.3 %all-to-all-start.1 = ((f32[2,1,3,32,128]{4,0,2,1,3:T(2,128)}), f32[2,1,3,32,128]{4,0,2,1,3:T(2,128)S(1)}, u32[]{:S(2)}, u32[]{:S(2)}) async-start(f32[2,1,3,32,128]{4,0,2,1,3:T(2,128)} %copy.197), calls=%async_computation.1 | async-start | bytes 196608 | tf_op jit(solution)/shard_map/all_to_all | solution.py:146
  513.7 14.4 %all-to-all-start.3 = ((f32[2,1,3,32,128]{4,0,2,1,3:T(2,128)}), f32[2,1,3,32,128]{4,0,2,1,3:T(2,128)S(1)}, u32[]{:S(2)}, u32[]{:S(2)}) async-start(f32[2,1,3,32,128]{4,0,2,1,3:T(2,128)} %copy.219), calls=%async_computation.3 | async-start | bytes 196608 | tf_op jit(solution)/shard_map/all_to_all | solution.py:146
  731.4 14.2 %all-to-all-start.5 = ((f32[2,1,3,32,128]{4,0,2,1,3:T(2,128)}), f32[2,1,3,32,128]{4,0,2,1,3:T(2,128)S(1)}, u32[]{:S(2)}, u32[]{:S(2)}) async-start(f32[2,1,3,32,128]{4,0,2,1,3:T(2,128)} %copy.241), calls=%async_computation.5 | async-start | bytes 196608 | tf_op jit(solution)/shard_map/all_to_all | solution.py:146
  748.6 127.9 %copy-start.2 = (f32[2,1,128,128]{3,2,1,0:T(8,128)}, f32[2,1,128,128]{3,2,1,0:T(8,128)S(1)}, u32[]{:S(2)}) copy-start(f32[2,1,128,128]{3,2,1,0:T(8,128)S(1)} %maximum_add_fusion.3) | copy-start | bytes 393220
